TPU v7x, 32 devices: a whole 2x2x4 slice. The times are simulated.
32 devices in a mesh: energy: 16 (over z, y, x), space: 2 (over core).
Axes of the slice: x: 2, y: 2, z: 4, core: 2. Of those that a mesh axis runs over, the one named last changes fastest.
Arguments:
- lesser: bfloat16 [32, 2, 2, 256, 256], P('energy', 'space'), may hold values from -6 to 6
- greater: bfloat16 [32, 2, 2, 256, 256], P('energy', 'space'), may hold values from -6 to 6
- coulomb_diag: bfloat16 [2, 256, 256], P('space'), may hold values from -0.375 to 0.375
- coulomb_upper: bfloat16 [2, 256, 256], P('space'), may hold values from -0.375 to 0.375
Outputs:
- screened: bfloat16 [32, 2, 2, 256, 256], P('energy', 'space')
All inputs are finite; a program needn't handle non-finite values.
Results may differ from a plain program's by a relative error of at most 0.015.
Values may be sent and summed in bfloat16 or wider, within the bound.
A program may use at most 64 MiB of HBM per device.

v0:
```python
import math
import jax
import jax.numpy as jnp
from jax import lax
from jax.sharding import PartitionSpec as P


def from_behind(value, axis, steps):
    count = lax.axis_size(axis)
    leading, last = (max(0, -steps), min(count, count - steps))
    return lax.ppermute(value, axis, [(source, source + steps) for source in range(leading, last)])


def split_parts(values):
    high = values.astype(jnp.bfloat16)
    low = (values - high.astype(jnp.float32)).astype(jnp.bfloat16)
    return (high, low)


def product_two(table, data_bf):
    return jnp.dot(table[0], data_bf, preferred_element_type=jnp.float32) + jnp.dot(
        table[1], data_bf, preferred_element_type=jnp.float32
    )


def product_three(table, data_f32):
    data_high, data_low = split_parts(data_f32)
    total = jnp.dot(table[0], data_high, preferred_element_type=jnp.float32)
    total = total + jnp.dot(table[1], data_high, preferred_element_type=jnp.float32)
    return total + jnp.dot(table[0], data_low, preferred_element_type=jnp.float32)


def correlate(lesser_x, greater_x):
    energies = lesser_x.shape[0]
    length = 2 * energies
    tail_shape = lesser_x.shape[1:]

    def flatten(values, part):
        return values[:, :, part].reshape(energies, -1)

    lesser_re = flatten(lesser_x, 0)
    lesser_im = flatten(lesser_x, 1)
    greater_re = flatten(greater_x, 0)
    greater_im = flatten(greater_x, 1)
    freqs = lax.broadcasted_iota(jnp.int32, (length, energies), 0)
    places = lax.broadcasted_iota(jnp.int32, (length, energies), 1)
    angles = 2.0 * math.pi / length * jnp.mod(freqs * places, length).astype(jnp.float32)
    cosine = split_parts(jnp.cos(angles))
    sine = split_parts(jnp.sin(angles))
    cosine_t = split_parts(jnp.cos(angles).T)
    sine_t = split_parts(jnp.sin(angles).T)
    hat_lre = product_two(cosine, lesser_re) + product_two(sine, lesser_im)
    hat_lim = product_two(cosine, lesser_im) - product_two(sine, lesser_re)
    hat_gre = product_two(cosine, greater_re) - product_two(sine, greater_im)
    hat_gim = product_two(cosine, greater_im) + product_two(sine, greater_re)
    prod_re = hat_lre * hat_gre - hat_lim * hat_gim
    prod_im = hat_lre * hat_gim + hat_lim * hat_gre
    corr_re = (product_three(cosine_t, prod_re) - product_three(sine_t, prod_im)) / length
    corr_im = (product_three(cosine_t, prod_im) + product_three(sine_t, prod_re)) / length
    factor = jnp.float32(energies) ** (-0.5)
    shaped = (energies, tail_shape[0], tail_shape[2], tail_shape[3])
    real_part = (corr_im * factor).reshape(shaped)
    imag_part = (-corr_re * factor).reshape(shaped)
    return jnp.stack([real_part, imag_part], axis=2).astype(jnp.bfloat16)


def left_plain(coupler, blocks):
    return jnp.einsum("ab,ecbd->ecad", coupler, blocks, preferred_element_type=jnp.float32).astype(
        jnp.bfloat16
    )


def left_transposed(coupler, blocks):
    return jnp.einsum("ba,ecbd->ecad", coupler, blocks, preferred_element_type=jnp.float32).astype(
        jnp.bfloat16
    )


def right_transposed(left, coupler):
    return jnp.einsum("ecad,fd->ecaf", left, coupler, preferred_element_type=jnp.float32)


def right_plain(left, coupler):
    return jnp.einsum("ecad,df->ecaf", left, coupler, preferred_element_type=jnp.float32)


def per_device(lesser, greater, coulomb_diag, coulomb_upper):
    greater_t = jnp.swapaxes(greater, 3, 4)
    lesser_x, greater_x = (
        lax.all_to_all(lesser, "energy", split_axis=3, concat_axis=0, tiled=True),
        lax.all_to_all(greater_t, "energy", split_axis=3, concat_axis=0, tiled=True),
    )
    polar_x = correlate(lesser_x, greater_x)
    polar = lax.all_to_all(polar_x, "energy", split_axis=0, concat_axis=3, tiled=True)
    own = polar[:, 0]
    diag_block = coulomb_diag[0]
    upper_block = coulomb_upper[0]
    total = right_transposed(left_plain(diag_block, own), diag_block)
    polar_next = from_behind(polar, "space", -1)
    outgoing = right_plain(left_transposed(upper_block, own), upper_block)
    total = total + right_transposed(left_plain(upper_block, polar_next[:, 0]), upper_block)
    incoming = from_behind(outgoing.astype(jnp.bfloat16), "space", 1).astype(outgoing.dtype)
    total = total + incoming
    return total.astype(jnp.bfloat16)[:, None]


def solution(mesh):
    placed = (
        P("energy", "space", None, None, None),
        P("energy", "space", None, None, None),
        P("space", None, None),
        P("space", None, None),
    )
    return jax.shard_map(
        per_device,
        mesh=mesh,
        in_specs=placed,
        out_specs=P("energy", "space", None, None, None),
        check_vma=False,
    )
```

profile of v0, /device:TPU:0, one launch (start us, length us, event | category | flops | bytes accessed | tf_op | source)
XLA Modules:
  0.0 81.9 jit_solution(16510284216522427563)
XLA Ops:
  0.0 2.0 %copy.27 = bf16[2,1,2,256,256]{3,2,0,1,4:T(2,128)(2,1)} copy(bf16[2,1,2,256,256]{4,3,2,1,0:T(8,128)(2,1)} %param.5) | data formatting | bytes 1048576 | tf_op args[1]
  2.0 8.5 %all-to-all-start.1 = ((bf16[2,1,2,256,256]{4,2,0,1,3:T(2,128)(2,1)}), bf16[2,1,2,256,256]{4,2,0,1,3:T(2,128)(2,1)S(1)}, u32[]{:S(2)}, u32[]{:S(2)}) async-start(bf16[2,1,2,256,256]{4,2,0,1,3:T(2,128)(2,1)} %bitcast.3), calls=%async_computation.1 | async-start | bytes 1048576 | tf_op jit(solution)/shard_map/all_to_all | solution.py:91
  10.5 1.3 %copy.24 = bf16[2,1,2,256,256]{4,2,0,1,3:T(2,128)(2,1)} copy(bf16[2,1,2,256,256]{4,3,2,1,0:T(8,128)(2,1)S(1)} %copy-done.4) | data formatting | bytes 1048576 | tf_op args[0]
  11.9 13.7 %all-to-all-done.1 = bf16[2,1,2,256,256]{4,2,0,1,3:T(2,128)(2,1)S(1)} async-done(((bf16[2,1,2,256,256]{4,2,0,1,3:T(2,128)(2,1)}), bf16[2,1,2,256,256]{4,2,0,1,3:T(2,128)(2,1)S(1)}, u32[]{:S(2)}, u32[]{:S(2)}) %all-to-all-start.1) | async-done | bytes 524320 | tf_op jit(solution)/shard_map/all_to_all | solution.py:91
  25.6 3.9 %all-to-all-start = ((bf16[2,1,2,256,256]{4,2,0,1,3:T(2,128)(2,1)}), bf16[2,1,2,256,256]{4,2,0,1,3:T(2,128)(2,1)S(1)}, u32[]{:S(2)}, u32[]{:S(2)}) async-start(bf16[2,1,2,256,256]{4,2,0,1,3:T(2,128)(2,1)} %copy.24), calls=%async_computation | async-start | bytes 1048576 | tf_op jit(solution)/shard_map/all_to_all | solution.py:90
  30.3 1.4 %fusion.48 = f32[64,4096]{1,0:T(8,128)} fusion(bf16[32,4096]{1,0:T(8,128)(2,1)S(1)} %bitcast.110), kind=kOutput, calls=%fused_computation.76 | convolution fusion | flops 16807936 | bytes 1310720 | tf_op jit(solution)/shard_map/dot_general | solution.py:21
  31.7 1.4 %fusion.52 = f32[64,4096]{1,0:T(8,128)} fusion(bf16[32,4096]{1,0:T(8,128)(2,1)S(1)} %bitcast.105), kind=kOutput, calls=%fused_computation.78 | convolution fusion | flops 16807936 | bytes 1310720 | tf_op jit(solution)/shard_map/dot_general | solution.py:21
  33.5 10.5 %all-to-all-done = bf16[2,1,2,256,256]{4,2,0,1,3:T(2,128)(2,1)S(1)} async-done(((bf16[2,1,2,256,256]{4,2,0,1,3:T(2,128)(2,1)}), bf16[2,1,2,256,256]{4,2,0,1,3:T(2,128)(2,1)S(1)}, u32[]{:S(2)}, u32[]{:S(2)}) %all-to-all-start) | async-done | bytes 524320 | tf_op jit(solution)/shard_map/all_to_all | solution.py:90
  45.9 0.4 copy-done.2
  46.4 0.4 convolution_add_fusion.5
  46.8 0.4 convolution_add_fusion.7
  47.2 0.8 copy-done.1
  48.0 0.4 convolution_add_fusion.1
  48.4 0.4 convolution_add_fusion.3
  48.8 0.4 fusion.2
  49.7 0.4 fusion
  50.1 0.6 multiply_add_fusion
  54.4 18.1 %all_to_all.54 = bf16[32,1,2,16,256]{4,3,2,1,0:T(8,128)(2,1)S(1)} all-to-all(bf16[32,1,2,16,256]{4,3,2,1,0:T(8,128)(2,1)S(1)} %pad_maximum_fusion), channel_id=1, replica_groups=mesh['energy'=16,'space'=2] {'energy'}, dimensions={0} | all-to-all | bytes 1048576 | tf_op jit(solution)/shard_map/all_to_all | solution.py:94
  72.7 1.3 %collective-permute-start = (bf16[2,1,2,256,256]{3,4,2,0,1:T(8,128)(2,1)S(1)}, bf16[2,1,2,256,256]{3,4,2,0,1:T(8,128)(2,1)S(1)}, u32[]{:S(2)}, u32[]{:S(2)}) collective-permute-start(bf16[2,1,2,256,256]{3,4,2,0,1:T(8,128)(2,1)S(1)} %copy.36), channel_id=1, source_target_pairs={{1,0},{3,2},{5,4},{7,6},{9,8},{11,10},{13,12},{15,14},{17,16},{19,... | collective-permute-start | bytes 1572872 | tf_op jit(solution)/shard_map/ppermute | solution.py:11
  74.0 1.6 %convolution_convert_fusion = bf16[2,2,256,256]{3,2,1,0:T(8,128)(2,1)} fusion(bf16[2,2,256,256]{3,2,1,0:T(8,128)(2,1)S(1)} %bitcast.122, bf16[1,256,256]{2,1,0:T(8,128)(2,1)S(1)} %copy-done), kind=kOutput, calls=%fused_computation.29 | convolution fusion | flops 268959744 | bytes 1179648 | tf_op jit(solution)/shard_map/ecad,df->ecaf/dot_general | solution.py:84
  75.6 3.1 %collective-permute-start.1 = (bf16[2,2,256,256]{3,2,1,0:T(8,128)(2,1)}, bf16[2,2,256,256]{3,2,1,0:T(8,128)(2,1)S(1)}, u32[]{:S(2)}, u32[]{:S(2)}) collective-permute-start(bf16[2,2,256,256]{3,2,1,0:T(8,128)(2,1)} %convolution_convert_fusion), channel_id=1, source_target_pairs={{0,1},{2,3},{4,5},{6,7},{8,9},{10,11},{12,13},{14,15},{16,17},{18,... | collective-permute-start | bytes 1572872 | tf_op jit(solution)/shard_map/ppermute | solution.py:11
  78.7 0.7 fusion.13
  79.4 1.0 %collective-permute-done.1 = bf16[2,2,256,256]{3,2,1,0:T(8,128)(2,1)S(1)} collective-permute-done((bf16[2,2,256,256]{3,2,1,0:T(8,128)(2,1)}, bf16[2,2,256,256]{3,2,1,0:T(8,128)(2,1)S(1)}, u32[]{:S(2)}, u32[]{:S(2)}) %collective-permute-start.1) | collective-permute-done | bytes 524320 | tf_op jit(solution)/shard_map/ppermute | solution.py:11
  80.4 1.5 %fusion.18 = bf16[2,1,2,256,256]{4,3,2,1,0:T(8,128)(2,1)} fusion(f32[2,2,256,256]{3,2,1,0:T(8,128)S(1)} %fusion.13, bf16[2,2,256,256]{3,2,1,0:T(8,128)(2,1)S(1)} %collective-permute-done.1, bf16[2,1,2,256,256]{3,4,2,0,1:T(8,128)(2,1)S(1)} %collective-permute-done, bf16[1,256,256]{2,1,0:T(8,128)(2,1)S(1)} %copy-done), kind=kOutput, calls=%fused_computation.39 | convolution fusion | flops 269746176 | bytes 2752512 | tf_op jit(solution)/shard_map/ecad,fd->ecaf/dot_general | solution.py:80
  (43 shorter events, 7.3 us)
Async XLA Ops:
  0.0 74.0 %copy-start = (bf16[1,256,256]{2,1,0:T(8,128)(2,1)S(1)}, bf16[1,256,256]{2,1,0:T(8,128)(2,1)}, u32[]{:S(2)}) copy-start(bf16[1,256,256]{2,1,0:T(8,128)(2,1)} %param.7) | copy-start | bytes 393220
  2.0 8.5 %copy-start.4 = (bf16[2,1,2,256,256]{4,3,2,1,0:T(8,128)(2,1)S(1)}, bf16[2,1,2,256,256]{4,3,2,1,0:T(8,128)(2,1)}, u32[]{:S(2)}) copy-start(bf16[2,1,2,256,256]{4,3,2,1,0:T(8,128)(2,1)} %param.4) | copy-start | bytes 1572868
  2.0 23.6 %all-to-all-start.1 = ((bf16[2,1,2,256,256]{4,2,0,1,3:T(2,128)(2,1)}), bf16[2,1,2,256,256]{4,2,0,1,3:T(2,128)(2,1)S(1)}, u32[]{:S(2)}, u32[]{:S(2)}) async-start(bf16[2,1,2,256,256]{4,2,0,1,3:T(2,128)(2,1)} %bitcast.3), calls=%async_computation.1 | async-start | bytes 1048576 | tf_op jit(solution)/shard_map/all_to_all | solution.py:91
  25.6 18.4 %all-to-all-start = ((bf16[2,1,2,256,256]{4,2,0,1,3:T(2,128)(2,1)}), bf16[2,1,2,256,256]{4,2,0,1,3:T(2,128)(2,1)S(1)}, u32[]{:S(2)}, u32[]{:S(2)}) async-start(bf16[2,1,2,256,256]{4,2,0,1,3:T(2,128)(2,1)} %copy.24), calls=%async_computation | async-start | bytes 1048576 | tf_op jit(solution)/shard_map/all_to_all | solution.py:90
  45.1 1.2 %copy-start.2 = (f32[64,4096]{1,0:T(8,128)S(1)}, f32[64,4096]{1,0:T(8,128)}, u32[]{:S(2)}) copy-start(f32[64,4096]{1,0:T(8,128)} %fusion.52) | copy-start | bytes 3145732
  46.8 1.2 %copy-start.1 = (f32[64,4096]{1,0:T(8,128)S(1)}, f32[64,4096]{1,0:T(8,128)}, u32[]{:S(2)}) copy-start(f32[64,4096]{1,0:T(8,128)} %fusion.48) | copy-start | bytes 3145732
  72.7 6.7 %collective-permute-start = (bf16[2,1,2,256,256]{3,4,2,0,1:T(8,128)(2,1)S(1)}, bf16[2,1,2,256,256]{3,4,2,0,1:T(8,128)(2,1)S(1)}, u32[]{:S(2)}, u32[]{:S(2)}) collective-permute-start(bf16[2,1,2,256,256]{3,4,2,0,1:T(8,128)(2,1)S(1)} %copy.36), channel_id=1, source_target_pairs={{1,0},{3,2},{5,4},{7,6},{9,8},{11,10},{13,12},{15,14},{17,16},{19,... | collective-permute-start | bytes 1572872 | tf_op jit(solution)/shard_map/ppermute | solution.py:11
  74.0 4.7 %copy-start.3 = (bf16[1,256,256]{2,1,0:T(8,128)(2,1)S(1)}, bf16[1,256,256]{2,1,0:T(8,128)(2,1)}, u32[]{:S(2)}) copy-start(bf16[1,256,256]{2,1,0:T(8,128)(2,1)} %param.6) | copy-start | bytes 393220
  75.6 4.8 %collective-permute-start.1 = (bf16[2,2,256,256]{3,2,1,0:T(8,128)(2,1)}, bf16[2,2,256,256]{3,2,1,0:T(8,128)(2,1)S(1)}, u32[]{:S(2)}, u32[]{:S(2)}) collective-permute-start(bf16[2,2,256,256]{3,2,1,0:T(8,128)(2,1)} %convolution_convert_fusion), channel_id=1, source_target_pairs={{0,1},{2,3},{4,5},{6,7},{8,9},{10,11},{12,13},{14,15},{16,17},{18,... | collective-permute-start | bytes 1572872 | tf_op jit(solution)/shard_map/ppermute | solution.py:11
where the time goes:
time: 82.4 us; the launch traced here: 81.9 us
  waiting for transfers between devices  25.2 us (31%)
  blocking collectives  18.1 us (22%)
  starting transfers between devices  16.8 us (20%)
  matrix products  15.8 us (19%)
  local copies, waits for them, and re-layouts  5.65 us (7%)
    all_to_all x1, blocking collectives, per_device(): lax.all_to_all(polar_x, 'energy', split_axis=0, concat_axis=3, tiled=True)  18.1 us
    all_to_all x1, waiting for transfers between devices, per_device(): lax.all_to_all(greater_t, 'energy', split_axis=3, concat_axis=0, tiled=True)  13.7 us
    all_to_all x1, waiting for transfers between devices, per_device(): lax.all_to_all(lesser, 'energy', split_axis=3, concat_axis=0, tiled=True)  10.5 us
    all_to_all x1, starting transfers between devices, per_device(): lax.all_to_all(greater_t, 'energy', split_axis=3, concat_axis=0, tiled=True)  8.47 us
    dot_general x8, matrix products, product_two(): jnp.dot(table[0], data_bf, preferred_element_type=jnp.float32)  5.1 us
    unnamed x18, local copies, waits for them, and re-layouts  5.07 us
    ppermute x2, starting transfers between devices, from_behind(): lax.ppermute(value, axis, [(source, source + steps) for source in range(l...  4.37 us
    all_to_all x1, starting transfers between devices, per_device(): lax.all_to_all(lesser, 'energy', split_axis=3, concat_axis=0, tiled=True)  3.95 us
  transfers between devices with their start and end apart: 4, of which 3 were waited for; matrix products, arithmetic and copies ran while one was open for 9% of the time, Pallas kernels for 0%

commit v1 on v0

--- a/solution.py
+++ b/solution.py
@@ -88,7 +88,12 @@
     greater_t = jnp.swapaxes(greater, 3, 4)
     lesser_x, greater_x = (
         lax.all_to_all(lesser, "energy", split_axis=3, concat_axis=0, tiled=True),
-        lax.all_to_all(greater_t, "energy", split_axis=3, concat_axis=0, tiled=True),
+        jnp.concatenate(
+            lax.all_to_all(
+                jnp.stack(jnp.split(greater_t, lax.axis_size("energy"), axis=3)), "energy", 0, 0
+            ),
+            axis=0,
+        ),
     )
     polar_x = correlate(lesser_x, greater_x)
     polar = lax.all_to_all(polar_x, "energy", split_axis=0, concat_axis=3, tiled=True)

time: 82.4 us -> 91.5 us (1.11)
  local copies, waits for them, and re-layouts: 5.65 us -> 14.6 us
    unnamed x18 -> x33, local copies, waits for them, and re-layouts: 5.07 us -> 13.6 us
  transfers between devices with their start and end apart: 4 -> 4, of which waited for: 3 -> 3; matrix products, arithmetic and copies ran while one was open for 9% -> 8% of each run, Pallas kernels for 0% -> 0%
where the time goes in v1:
time: 91.5 us; the launch traced here: 91 us
  waiting for transfers between devices  25.3 us (28%)
  blocking collectives  18.1 us (20%)
  starting transfers between devices  16.8 us (18%)
  matrix products  15.8 us (17%)
  local copies, waits for them, and re-layouts  14.6 us (16%)
    all_to_all x1, blocking collectives, per_device(): lax.all_to_all(polar_x, 'energy', split_axis=0, concat_axis=3, tiled=True)  18.1 us
    all_to_all x1, waiting for transfers between devices, per_device(): lax.all_to_all(jnp.stack(jnp.split(greater_t, lax.axis_size('energy'), ax...  13.7 us
    unnamed x33, local copies, waits for them, and re-layouts  13.6 us
    all_to_all x1, waiting for transfers between devices, per_device(): lax.all_to_all(lesser, 'energy', split_axis=3, concat_axis=0, tiled=True)  10.6 us
    all_to_all x1, starting transfers between devices, per_device(): lax.all_to_all(jnp.stack(jnp.split(greater_t, lax.axis_size('energy'), ax...  8.47 us
    dot_general x8, matrix products, product_two(): jnp.dot(table[0], data_bf, preferred_element_type=jnp.float32)  5.1 us
    ppermute x2, starting transfers between devices, from_behind(): lax.ppermute(value, axis, [(source, source + steps) for source in range(l...  4.37 us
    all_to_all x1, starting transfers between devices, per_device(): lax.all_to_all(lesser, 'energy', split_axis=3, concat_axis=0, tiled=True)  3.95 us
  transfers between devices with their start and end apart: 4, of which 3 were waited for; matrix products, arithmetic and copies ran while one was open for 8% of the time, Pallas kernels for 0%

profile of v1, /device:TPU:0, one launch (start us, length us, event | category | flops | bytes accessed | tf_op | source)
XLA Modules:
  0.0 91.0 jit_solution(9685016011702220772)
XLA Ops:
  0.0 1.3 %copy.72 = bf16[2,1,2,256,256]{3,4,2,0,1:T(8,128)(2,1)S(1)} copy(bf16[2,1,2,256,256]{4,3,2,1,0:T(8,128)(2,1)} %param.5) | data formatting | bytes 1048576 | tf_op args[1]
  1.3 0.6 constant_dynamic-update-slice_fusion.15
  1.9 0.6 constant_dynamic-update-slice_fusion.14
  2.5 0.6 constant_dynamic-update-slice_fusion.13
  3.1 0.6 constant_dynamic-update-slice_fusion.12
  3.8 0.6 constant_dynamic-update-slice_fusion.11
  4.4 0.6 constant_dynamic-update-slice_fusion.10
  7.5 0.6 constant_dynamic-update-slice_fusion.5
  11.2 8.5 %all-to-all-start.1 = ((bf16[16,2,1,2,16,256]{5,4,3,2,1,0:T(8,128)(2,1)}), bf16[16,2,1,2,16,256]{5,4,3,2,1,0:T(8,128)(2,1)S(1)}, u32[]{:S(2)}, u32[]{:S(2)}) async-start(bf16[16,2,1,2,16,256]{5,4,3,2,1,0:T(8,128)(2,1)} %constant_dynamic-update-slice_fusion), calls=%async_computation.1 | async-start | bytes 1048576 | tf_op jit(solution)/shard_map/all_to_all | solution.py:92
  19.7 1.3 %copy.69 = bf16[2,1,2,256,256]{4,2,0,1,3:T(2,128)(2,1)} copy(bf16[2,1,2,256,256]{4,3,2,1,0:T(8,128)(2,1)S(1)} %copy-done.4) | data formatting | bytes 1048576 | tf_op args[0]
  21.0 13.7 %all-to-all-done.1 = bf16[16,2,1,2,16,256]{5,4,3,2,1,0:T(8,128)(2,1)S(1)} async-done(((bf16[16,2,1,2,16,256]{5,4,3,2,1,0:T(8,128)(2,1)}), bf16[16,2,1,2,16,256]{5,4,3,2,1,0:T(8,128)(2,1)S(1)}, u32[]{:S(2)}, u32[]{:S(2)}) %all-to-all-start.1) | async-done | bytes 524320 | tf_op jit(solution)/shard_map/all_to_all | solution.py:92
  34.7 3.9 %all-to-all-start = ((bf16[2,1,2,256,256]{4,2,0,1,3:T(2,128)(2,1)}), bf16[2,1,2,256,256]{4,2,0,1,3:T(2,128)(2,1)S(1)}, u32[]{:S(2)}, u32[]{:S(2)}) async-start(bf16[2,1,2,256,256]{4,2,0,1,3:T(2,128)(2,1)} %copy.69), calls=%async_computation | async-start | bytes 1048576 | tf_op jit(solution)/shard_map/all_to_all | solution.py:90
  39.3 1.4 %fusion.48 = f32[64,4096]{1,0:T(8,128)} fusion(bf16[32,4096]{1,0:T(8,128)(2,1)S(1)} %bitcast.203), kind=kOutput, calls=%fused_computation.108 | convolution fusion | flops 16807936 | bytes 1310720 | tf_op jit(solution)/shard_map/dot_general | solution.py:21
  40.7 1.4 %fusion.52 = f32[64,4096]{1,0:T(8,128)} fusion(bf16[32,4096]{1,0:T(8,128)(2,1)S(1)} %bitcast.198), kind=kOutput, calls=%fused_computation.110 | convolution fusion | flops 16807936 | bytes 1310720 | tf_op jit(solution)/shard_map/dot_general | solution.py:21
  42.5 10.6 %all-to-all-done = bf16[2,1,2,256,256]{4,2,0,1,3:T(2,128)(2,1)S(1)} async-done(((bf16[2,1,2,256,256]{4,2,0,1,3:T(2,128)(2,1)}), bf16[2,1,2,256,256]{4,2,0,1,3:T(2,128)(2,1)S(1)}, u32[]{:S(2)}, u32[]{:S(2)}) %all-to-all-start) | async-done | bytes 524320 | tf_op jit(solution)/shard_map/all_to_all | solution.py:90
  55.9 0.8 copy-done.1
  59.2 0.6 multiply_add_fusion
  63.5 18.1 %all_to_all.41 = bf16[32,1,2,16,256]{4,3,2,1,0:T(8,128)(2,1)S(1)} all-to-all(bf16[32,1,2,16,256]{4,3,2,1,0:T(8,128)(2,1)S(1)} %pad_maximum_fusion), channel_id=1, replica_groups=mesh['energy'=16,'space'=2] {'energy'}, dimensions={0} | all-to-all | bytes 1048576 | tf_op jit(solution)/shard_map/all_to_all | solution.py:99
  81.9 1.3 %collective-permute-start = (bf16[2,1,2,256,256]{3,4,2,0,1:T(8,128)(2,1)S(1)}, bf16[2,1,2,256,256]{3,4,2,0,1:T(8,128)(2,1)S(1)}, u32[]{:S(2)}, u32[]{:S(2)}) collective-permute-start(bf16[2,1,2,256,256]{3,4,2,0,1:T(8,128)(2,1)S(1)} %copy.96), channel_id=1, source_target_pairs={{1,0},{3,2},{5,4},{7,6},{9,8},{11,10},{13,12},{15,14},{17,16},{19,... | collective-permute-start | bytes 1572872 | tf_op jit(solution)/shard_map/ppermute | solution.py:11
  83.2 1.6 %convolution_convert_fusion = bf16[2,2,256,256]{3,2,1,0:T(8,128)(2,1)} fusion(bf16[2,2,256,256]{3,2,1,0:T(8,128)(2,1)S(1)} %bitcast.215, bf16[1,256,256]{2,1,0:T(8,128)(2,1)S(1)} %copy-done), kind=kOutput, calls=%fused_computation.29 | convolution fusion | flops 268959744 | bytes 1179648 | tf_op jit(solution)/shard_map/ecad,df->ecaf/dot_general | solution.py:84
  84.7 3.1 %collective-permute-start.1 = (bf16[2,2,256,256]{3,2,1,0:T(8,128)(2,1)}, bf16[2,2,256,256]{3,2,1,0:T(8,128)(2,1)S(1)}, u32[]{:S(2)}, u32[]{:S(2)}) collective-permute-start(bf16[2,2,256,256]{3,2,1,0:T(8,128)(2,1)} %convolution_convert_fusion), channel_id=1, source_target_pairs={{0,1},{2,3},{4,5},{6,7},{8,9},{10,11},{12,13},{14,15},{16,17},{18,... | collective-permute-start | bytes 1572872 | tf_op jit(solution)/shard_map/ppermute | solution.py:11
  87.8 0.7 fusion.13
  88.6 1.0 %collective-permute-done.1 = bf16[2,2,256,256]{3,2,1,0:T(8,128)(2,1)S(1)} collective-permute-done((bf16[2,2,256,256]{3,2,1,0:T(8,128)(2,1)}, bf16[2,2,256,256]{3,2,1,0:T(8,128)(2,1)S(1)}, u32[]{:S(2)}, u32[]{:S(2)}) %collective-permute-start.1) | collective-permute-done | bytes 524320 | tf_op jit(solution)/shard_map/ppermute | solution.py:11
  89.5 1.5 %fusion.18 = bf16[2,1,2,256,256]{4,3,2,1,0:T(8,128)(2,1)} fusion(f32[2,2,256,256]{3,2,1,0:T(8,128)S(1)} %fusion.13, bf16[2,2,256,256]{3,2,1,0:T(8,128)(2,1)S(1)} %collective-permute-done.1, bf16[2,1,2,256,256]{3,4,2,0,1:T(8,128)(2,1)S(1)} %collective-permute-done, bf16[1,256,256]{2,1,0:T(8,128)(2,1)S(1)} %copy-done), kind=kOutput, calls=%fused_computation.39 | convolution fusion | flops 269746176 | bytes 2752512 | tf_op jit(solution)/shard_map/ecad,fd->ecaf/dot_general | solution.py:80
  (57 shorter events, 15.6 us)
Async XLA Ops:
  0.0 83.2 %copy-start = (bf16[1,256,256]{2,1,0:T(8,128)(2,1)S(1)}, bf16[1,256,256]{2,1,0:T(8,128)(2,1)}, u32[]{:S(2)}) copy-start(bf16[1,256,256]{2,1,0:T(8,128)(2,1)} %param.7) | copy-start | bytes 393220
  11.2 8.5 %copy-start.4 = (bf16[2,1,2,256,256]{4,3,2,1,0:T(8,128)(2,1)S(1)}, bf16[2,1,2,256,256]{4,3,2,1,0:T(8,128)(2,1)}, u32[]{:S(2)}) copy-start(bf16[2,1,2,256,256]{4,3,2,1,0:T(8,128)(2,1)} %param.4) | copy-start | bytes 1572868
  11.2 23.6 %all-to-all-start.1 = ((bf16[16,2,1,2,16,256]{5,4,3,2,1,0:T(8,128)(2,1)}), bf16[16,2,1,2,16,256]{5,4,3,2,1,0:T(8,128)(2,1)S(1)}, u32[]{:S(2)}, u32[]{:S(2)}) async-start(bf16[16,2,1,2,16,256]{5,4,3,2,1,0:T(8,128)(2,1)} %constant_dynamic-update-slice_fusion), calls=%async_computation.1 | async-start | bytes 1048576 | tf_op jit(solution)/shard_map/all_to_all | solution.py:92
  34.7 18.4 %all-to-all-start = ((bf16[2,1,2,256,256]{4,2,0,1,3:T(2,128)(2,1)}), bf16[2,1,2,256,256]{4,2,0,1,3:T(2,128)(2,1)S(1)}, u32[]{:S(2)}, u32[]{:S(2)}) async-start(bf16[2,1,2,256,256]{4,2,0,1,3:T(2,128)(2,1)} %copy.69), calls=%async_computation | async-start | bytes 1048576 | tf_op jit(solution)/shard_map/all_to_all | solution.py:90
  54.3 1.2 %copy-start.2 = (f32[64,4096]{1,0:T(8,128)S(1)}, f32[64,4096]{1,0:T(8,128)}, u32[]{:S(2)}) copy-start(f32[64,4096]{1,0:T(8,128)} %fusion.52) | copy-start | bytes 3145732
  55.5 1.2 %copy-start.1 = (f32[64,4096]{1,0:T(8,128)S(1)}, f32[64,4096]{1,0:T(8,128)}, u32[]{:S(2)}) copy-start(f32[64,4096]{1,0:T(8,128)} %fusion.48) | copy-start | bytes 3145732
  81.9 6.7 %collective-permute-start = (bf16[2,1,2,256,256]{3,4,2,0,1:T(8,128)(2,1)S(1)}, bf16[2,1,2,256,256]{3,4,2,0,1:T(8,128)(2,1)S(1)}, u32[]{:S(2)}, u32[]{:S(2)}) collective-permute-start(bf16[2,1,2,256,256]{3,4,2,0,1:T(8,128)(2,1)S(1)} %copy.96), channel_id=1, source_target_pairs={{1,0},{3,2},{5,4},{7,6},{9,8},{11,10},{13,12},{15,14},{17,16},{19,... | collective-permute-start | bytes 1572872 | tf_op jit(solution)/shard_map/ppermute | solution.py:11
  83.2 4.7 %copy-start.3 = (bf16[1,256,256]{2,1,0:T(8,128)(2,1)S(1)}, bf16[1,256,256]{2,1,0:T(8,128)(2,1)}, u32[]{:S(2)}) copy-start(bf16[1,256,256]{2,1,0:T(8,128)(2,1)} %param.6) | copy-start | bytes 393220
  84.7 4.8 %collective-permute-start.1 = (bf16[2,2,256,256]{3,2,1,0:T(8,128)(2,1)}, bf16[2,2,256,256]{3,2,1,0:T(8,128)(2,1)S(1)}, u32[]{:S(2)}, u32[]{:S(2)}) collective-permute-start(bf16[2,2,256,256]{3,2,1,0:T(8,128)(2,1)} %convolution_convert_fusion), channel_id=1, source_target_pairs={{0,1},{2,3},{4,5},{6,7},{8,9},{10,11},{12,13},{14,15},{16,17},{18,... | collective-permute-start | bytes 1572872 | tf_op jit(solution)/shard_map/ppermute | solution.py:11
